TPU v7x, 256 devices: a whole 4x4x8 slice. The times are simulated.
256 devices in a mesh: row: 8 (over y, core), col: 32 (over z, x).
Axes of the slice: x: 4, y: 4, z: 8, core: 2. Of those that a mesh axis runs over, the one named last changes fastest.
Arguments:
- embeds: bfloat16 [3072, 8192], P('row', 'col'), may hold values from -600 to 600
- ln_gain: float32 [8192], replicated, may hold values from 0.1 to 1.9
- ln_bias: float32 [8192], replicated, may hold values from -3 to 3
- w_qkv: bfloat16 [8192, 24576], P('row', 'col'), may hold values from -4 to 4, as said below
- w_out: bfloat16 [8192, 8192], P('row', 'col'), may hold values from -0.0625 to 0.0625
- out_bias: float32 [8192], P('col'), may hold values from -3 to 3
Outputs:
- attended: bfloat16 [3072, 8192], P('row', 'col')
Inputs may be any that keep to these rules, and one draw needn't show every extreme that they name: Columns of w_qkv are ordered by head, then query, key, value, then entry of the head.
All inputs are finite; a program needn't handle non-finite values.
Results may differ from a plain program's by a relative error of at most 0.0065.
Values may be sent and summed in bfloat16 or wider, within the bound.
A program may use at most 64 MiB of HBM per device.

v0:
```python
import jax
import jax.numpy as jnp
from jax import lax
from jax.sharding import PartitionSpec as P

D = 8192
HEADS = 64
SEQ = 128


def normalize(values, mean, var, gain, shift):
    return ((values - mean) * lax.rsqrt(var + 1e-05) * gain + shift).astype(jnp.bfloat16)


def attend(qkv):
    total, columns = qkv.shape
    head_size = D // HEADS
    heads = columns // (3 * head_size)
    packed = qkv.reshape(total // SEQ, SEQ, heads, 3, head_size)
    query = packed[:, :, :, 0]
    keys = packed[:, :, :, 1]
    vals = packed[:, :, :, 2]
    scores = jnp.einsum("nqhd,nkhd->nhqk", query, keys, preferred_element_type=jnp.float32)
    scores = scores / jnp.sqrt(jnp.float32(head_size))
    peak = jnp.max(scores, axis=-1, keepdims=True)
    expo = jnp.exp(scores - peak)
    probs = (expo / jnp.sum(expo, axis=-1, keepdims=True)).astype(jnp.bfloat16)
    context = jnp.einsum("nhqk,nkhd->nqhd", probs, vals, preferred_element_type=jnp.float32)
    return context.astype(jnp.bfloat16).reshape(total, heads * head_size)


def on_device(embeds, ln_gain, ln_bias, w_qkv, w_out, out_bias):
    width = embeds.shape[1]
    offset = lax.axis_index("col") * width
    values = embeds.astype(jnp.float32)
    gain_part = lax.dynamic_slice_in_dim(ln_gain, offset, width)
    bias_part = lax.dynamic_slice_in_dim(ln_bias, offset, width)
    mean = lax.psum(jnp.sum(values, axis=1), "col")[:, None] / D
    spread = lax.psum(jnp.sum((values - mean) ** 2, axis=1), "col")
    payload = normalize(values, mean, spread[:, None] / D, gain_part, bias_part)
    gathered = lax.all_gather(payload, "col", axis=1, tiled=True)
    left = gathered
    qkv = jnp.dot(
        left, lax.all_gather(w_qkv, "row", axis=0, tiled=True), preferred_element_type=jnp.float32
    )
    context = attend(qkv.astype(jnp.bfloat16))
    full_context = lax.all_gather(context, "col", axis=1, tiled=True)
    left = full_context
    result = jnp.dot(
        left, lax.all_gather(w_out, "row", axis=0, tiled=True), preferred_element_type=jnp.float32
    )
    return (result + out_bias).astype(jnp.bfloat16)


def solution(mesh):
    return jax.shard_map(
        on_device,
        mesh=mesh,
        in_specs=(P("row", "col"), P(), P(), P("row", "col"), P("row", "col"), P("col")),
        out_specs=P("row", "col"),
        check_vma=False,
    )
```

profile of v0, /device:TPU:36, one launch (start us, length us, event | category | flops | bytes accessed | tf_op | source)
XLA Modules:
  0.0 465.9 jit_solution(14634312466143647871)
XLA Ops:
  6.5 0.8 dynamic_slice.6
  7.3 0.8 dynamic_slice.7
  8.1 1.1 convert_reduce_fusion
  9.1 66.9 %psum.14 = f32[384]{0:T(512)S(1)} all-reduce(f32[384]{0:T(512)S(1)} %convert_reduce_fusion), channel_id=1, replica_groups=mesh['row'=8,'col'=32] {'col'}, use_global_device_ids=true, to_apply=%region_1.0 | all-reduce | flops 384 | bytes 3072 | tf_op jit(solution)/shard_map/psum | solution.py:38
  76.0 1.2 fusion.7
  77.2 69.6 %psum.15 = f32[384]{0:T(512)S(1)} all-reduce(f32[384]{0:T(512)S(1)} %fusion.7), channel_id=1, replica_groups=mesh['row'=8,'col'=32] {'col'}, use_global_device_ids=true, to_apply=%region_3.0 | all-reduce | flops 384 | bytes 3072 | tf_op jit(solution)/shard_map/psum | solution.py:39
  146.8 1.8 fusion.10
  148.6 0.0 all-gather.7.cloned.1.call-start
  148.7 0.7 all-gather.7.cloned.1.call-update
  149.4 0.7 all-gather.11.cloned.1.call-update
  150.2 98.9 %all-gather.5.cloned.1.call-done = bf16[384,8192]{1,0:T(8,128)(2,1)} async-done(((bf16[384,256]{1,0:T(8,128)(2,1)}), bf16[384,8192]{1,0:T(8,128)(2,1)}) %all-gather.5.cloned.1.call-update) | async-done | bytes 6291472 | tf_op jit(solution)/shard_map/all_gather | solution.py:41
  249.1 70.9 %all-gather.7.cloned.1.call-done = bf16[8192,768]{1,0:T(8,128)(2,1)} async-done(((bf16[1024,768]{1,0:T(8,128)(2,1)}), bf16[8192,768]{1,0:T(8,128)(2,1)}) %all-gather.7.cloned.1.call-update) | async-done | bytes 12582928 | tf_op jit(solution)/shard_map/all_gather | solution.py:44
  320.0 10.8 %convolution_convert_fusion = bf16[384,768]{1,0:T(8,128)(2,1)S(1)} fusion(bf16[384,8192]{1,0:T(8,128)(2,1)} %all-gather.5.cloned.1.call-done, bf16[8192,768]{1,0:T(8,128)(2,1)} %all-gather.7.cloned.1.call-done), kind=kOutput, calls=%fused_computation.1 | convolution fusion | flops 4832133120 | bytes 19464192 | tf_op jit(solution)/shard_map/dot_general | solution.py:43
  330.8 0.3 reshape.17
  331.1 0.9 fusion.15
  332.0 0.6 copy.17
  332.6 0.3 fusion.16
  332.9 0.3 convolution_multiply_fusion
  333.1 0.3 fusion.4
  333.4 0.2 copy.15
  333.6 0.7 copy.34
  334.3 22.6 %all-gather.11.cloned.1.call-done = bf16[8192,256]{1,0:T(8,128)(2,1)} async-done(((bf16[1024,256]{1,0:T(8,128)(2,1)}), bf16[8192,256]{1,0:T(8,128)(2,1)}) %all-gather.11.cloned.1.call-update) | async-done | bytes 4194320 | tf_op jit(solution)/shard_map/all_gather | solution.py:50
  356.9 96.0 %all-gather.9.cloned.1.call-done = bf16[384,8192]{1,0:T(8,128)(2,1)} async-done(((bf16[384,256]{1,0:T(8,128)(2,1)}), bf16[384,8192]{1,0:T(8,128)(2,1)}) %all-gather.9.cloned.1.call-update) | async-done | bytes 6291472 | tf_op jit(solution)/shard_map/all_gather | solution.py:47
  452.9 6.5 %fusion.3 = bf16[384,256]{1,0:T(8,128)(2,1)} fusion(bf16[384,8192]{1,0:T(8,128)(2,1)} %all-gather.9.cloned.1.call-done, bf16[8192,256]{1,0:T(8,128)(2,1)} %all-gather.11.cloned.1.call-done, f32[256]{0:T(256)S(1)} %copy-done), kind=kOutput, calls=%fused_computation.6 | convolution fusion | flops 1610809344 | bytes 10683392 | tf_op jit(solution)/shard_map/dot_general | solution.py:49
  (9 shorter events, 0.1 us)
Async XLA Ops:
  6.5 242.5 %all-gather.5.cloned.1.call-start = ((), (), s32[]{:S(2)}) async-start(), calls=%async_computation | async-start | bytes 6488064 | tf_op jit(solution)/shard_map/all_gather | solution.py:41
  148.6 171.4 %all-gather.7.cloned.1.call-start = ((), (), s32[]{:S(2)}) async-start(), calls=%async_computation.1 | async-start | bytes 14155776 | tf_op jit(solution)/shard_map/all_gather | solution.py:44
  149.4 207.5 %all-gather.11.cloned.1.call-start = ((), (), s32[]{:S(2)}) async-start(), calls=%async_computation.3 | async-start | bytes 4718592 | tf_op jit(solution)/shard_map/all_gather | solution.py:50
  150.1 302.8 %all-gather.9.cloned.1.call-start = ((), (), s32[]{:S(2)}) async-start(), calls=%async_computation.2 | async-start | bytes 6488064 | tf_op jit(solution)/shard_map/all_gather | solution.py:47
  330.8 122.1 %copy-start = (f32[256]{0:T(256)S(1)}, f32[256]{0:T(256)}, u32[]{:S(2)}) copy-start(f32[256]{0:T(256)} %param.11) | copy-start | bytes 3076
Sparse Core Ops, SparseCore 0:
  148.7 100.2 all-gather.4
  250.9 69.0 all-gather.6
  321.9 35.0 all-gather.10
  359.2 93.6 all-gather.8
where the time goes:
time: 466 us
  waiting for transfers between devices  290 us (62%)
  blocking collectives  137 us (29%)
  matrix products  18.1 us (4%)
  between operations  13.2 us (3%)
    all_gather x1, waiting for transfers between devices, on_device(): gathered = lax.all_gather(payload, 'col', axis=1, tiled=True)  98.9 us
    all_gather x1, waiting for transfers between devices, on_device(): full_context = lax.all_gather(context, 'col', axis=1, tiled=True)  96 us
    all_gather x1, waiting for transfers between devices, on_device(): lax.all_gather(w_qkv, 'row', axis=0, tiled=True)  70.9 us
    psum x1, blocking collectives, on_device(): spread = lax.psum(jnp.sum((values - mean) ** 2, axis=1), 'col')  69.6 us
    psum x1, blocking collectives, on_device(): mean = lax.psum(jnp.sum(values, axis=1), 'col')[:, None] / D  66.9 us
    all_gather x1, waiting for transfers between devices, on_device(): lax.all_gather(w_out, 'row', axis=0, tiled=True)  22.6 us
    dot_general x1, matrix products, on_device(): jnp.dot(left, lax.all_gather(w_qkv, 'row', axis=0, tiled=True), preferred...  10.8 us
  transfers between devices with their start and end apart: 4, of which 4 were waited for; matrix products, arithmetic and copies ran while one was open for 3% of the time, Pallas kernels for 0%

commit v1 on v0

--- a/solution.py
+++ b/solution.py
@@ -35,7 +35,7 @@
     values = embeds.astype(jnp.float32)
     gain_part = lax.dynamic_slice_in_dim(ln_gain, offset, width)
     bias_part = lax.dynamic_slice_in_dim(ln_bias, offset, width)
-    mean = lax.psum(jnp.sum(values, axis=1), "col")[:, None] / D
+    mean = jnp.sum(lax.all_gather(jnp.sum(values, axis=1), "col"), axis=0)[:, None] / D
     spread = lax.psum(jnp.sum((values - mean) ** 2, axis=1), "col")
     payload = normalize(values, mean, spread[:, None] / D, gain_part, bias_part)
     gathered = lax.all_gather(payload, "col", axis=1, tiled=True)

time: 466 us -> 442 us (0.948)
  blocking collectives: 137 us -> 112 us
    psum x1 -> x0, blocking collectives: 66.9 us -> none  [on_device(): mean = lax.psum(jnp.sum(values, axis=1), 'col')[:, None] / D]
    all_gather x0 -> x1, blocking collectives: none -> 47.2 us  [on_device(): lax.all_gather(jnp.sum(values, axis=1), 'col')]
where the time goes in v1:
time: 442 us; the launch traced here: 441 us
  waiting for transfers between devices  289 us (65%)
  blocking collectives  112 us (25%)
  matrix products  18.1 us (4%)
  between operations  13.2 us (3%)
    all_gather x1, waiting for transfers between devices, on_device(): gathered = lax.all_gather(payload, 'col', axis=1, tiled=True)  98.4 us
    all_gather x1, waiting for transfers between devices, on_device(): full_context = lax.all_gather(context, 'col', axis=1, tiled=True)  96 us
    all_gather x1, waiting for transfers between devices, on_device(): lax.all_gather(w_qkv, 'row', axis=0, tiled=True)  70.9 us
    psum x1, blocking collectives, on_device(): spread = lax.psum(jnp.sum((values - mean) ** 2, axis=1), 'col')  65.2 us
    all_gather x1, blocking collectives, on_device(): lax.all_gather(jnp.sum(values, axis=1), 'col')  47.2 us
    all_gather x1, waiting for transfers between devices, on_device(): lax.all_gather(w_out, 'row', axis=0, tiled=True)  22.6 us
    dot_general x1, matrix products, on_device(): jnp.dot(left, lax.all_gather(w_qkv, 'row', axis=0, tiled=True), preferred...  10.8 us
  transfers between devices with their start and end apart: 4, of which 4 were waited for; matrix products, arithmetic and copies ran while one was open for 3% of the time, Pallas kernels for 0%

profile of v1, /device:TPU:36, one launch (start us, length us, event | category | flops | bytes accessed | tf_op | source)
XLA Modules:
  0.0 441.3 jit_solution(13702997916825083631)
XLA Ops:
  6.5 0.8 dynamic_slice.6
  7.3 0.8 dynamic_slice.7
  8.1 1.1 convert_reduce_fusion
  9.1 47.2 %all-gather.1 = f32[32,1,384]{2,1,0:T(1,128)S(1)} all-gather(f32[1,1,384]{2,1,0:T(1,128)S(1)} %reshape.22), channel_id=2, replica_groups=mesh['row'=8,'col'=32] {'col'}, dimensions={0}, use_global_device_ids=true | all-gather | bytes 50688 | tf_op jit(solution)/shard_map/all_gather | solution.py:38
  56.3 0.1 reduce_sum.37
  56.4 1.2 fusion.7
  57.5 65.2 %psum.7 = f32[384]{0:T(512)S(1)} all-reduce(f32[384]{0:T(512)S(1)} %fusion.7), channel_id=1, replica_groups=mesh['row'=8,'col'=32] {'col'}, use_global_device_ids=true, to_apply=%region_3.0 | all-reduce | flops 384 | bytes 3072 | tf_op jit(solution)/shard_map/psum | solution.py:39
  122.7 1.8 fusion.10
  124.6 0.7 all-gather.9.cloned.1.call-update
  125.3 0.7 all-gather.13.cloned.1.call-update
  126.1 98.4 %all-gather.7.cloned.1.call-done = bf16[384,8192]{1,0:T(8,128)(2,1)} async-done(((bf16[384,256]{1,0:T(8,128)(2,1)}), bf16[384,8192]{1,0:T(8,128)(2,1)}) %all-gather.7.cloned.1.call-update) | async-done | bytes 6291472 | tf_op jit(solution)/shard_map/all_gather | solution.py:41
  224.4 70.9 %all-gather.9.cloned.1.call-done = bf16[8192,768]{1,0:T(8,128)(2,1)} async-done(((bf16[1024,768]{1,0:T(8,128)(2,1)}), bf16[8192,768]{1,0:T(8,128)(2,1)}) %all-gather.9.cloned.1.call-update) | async-done | bytes 12582928 | tf_op jit(solution)/shard_map/all_gather | solution.py:44
  295.4 10.8 %convolution_convert_fusion = bf16[384,768]{1,0:T(8,128)(2,1)S(1)} fusion(bf16[384,8192]{1,0:T(8,128)(2,1)} %all-gather.7.cloned.1.call-done, bf16[8192,768]{1,0:T(8,128)(2,1)} %all-gather.9.cloned.1.call-done), kind=kOutput, calls=%fused_computation.1 | convolution fusion | flops 4832133120 | bytes 19464192 | tf_op jit(solution)/shard_map/dot_general | solution.py:43
  306.2 0.3 reshape.19
  306.5 0.9 fusion.15
  307.3 0.6 copy.22
  307.9 0.3 fusion.16
  308.2 0.3 convolution_multiply_fusion
  308.5 0.3 fusion.4
  308.8 0.2 copy.20
  308.9 0.7 copy.39
  309.7 22.6 %all-gather.13.cloned.1.call-done = bf16[8192,256]{1,0:T(8,128)(2,1)} async-done(((bf16[1024,256]{1,0:T(8,128)(2,1)}), bf16[8192,256]{1,0:T(8,128)(2,1)}) %all-gather.13.cloned.1.call-update) | async-done | bytes 4194320 | tf_op jit(solution)/shard_map/all_gather | solution.py:50
  332.3 96.0 %all-gather.11.cloned.1.call-done = bf16[384,8192]{1,0:T(8,128)(2,1)} async-done(((bf16[384,256]{1,0:T(8,128)(2,1)}), bf16[384,8192]{1,0:T(8,128)(2,1)}) %all-gather.11.cloned.1.call-update) | async-done | bytes 6291472 | tf_op jit(solution)/shard_map/all_gather | solution.py:47
  428.3 6.5 %fusion.3 = bf16[384,256]{1,0:T(8,128)(2,1)} fusion(bf16[384,8192]{1,0:T(8,128)(2,1)} %all-gather.11.cloned.1.call-done, bf16[8192,256]{1,0:T(8,128)(2,1)} %all-gather.13.cloned.1.call-done, f32[256]{0:T(256)S(1)} %copy-done), kind=kOutput, calls=%fused_computation.6 | convolution fusion | flops 1610809344 | bytes 10683392 | tf_op jit(solution)/shard_map/dot_general | solution.py:49
  (11 shorter events, 0.2 us)
Async XLA Ops:
  6.5 217.9 %all-gather.7.cloned.1.call-start = ((), (), s32[]{:S(2)}) async-start(), calls=%async_computation | async-start | bytes 6488064 | tf_op jit(solution)/shard_map/all_gather | solution.py:41
  124.5 170.8 %all-gather.9.cloned.1.call-start = ((), (), s32[]{:S(2)}) async-start(), calls=%async_computation.1 | async-start | bytes 14155776 | tf_op jit(solution)/shard_map/all_gather | solution.py:44
  125.3 207.0 %all-gather.13.cloned.1.call-start = ((), (), s32[]{:S(2)}) async-start(), calls=%async_computation.3 | async-start | bytes 4718592 | tf_op jit(solution)/shard_map/all_gather | solution.py:50
  126.0 302.3 %all-gather.11.cloned.1.call-start = ((), (), s32[]{:S(2)}) async-start(), calls=%async_computation.2 | async-start | bytes 6488064 | tf_op jit(solution)/shard_map/all_gather | solution.py:47
  306.1 122.2 %copy-start = (f32[256]{0:T(256)S(1)}, f32[256]{0:T(256)}, u32[]{:S(2)}) copy-start(f32[256]{0:T(256)} %param.11) | copy-start | bytes 3076
Sparse Core Ops, SparseCore 0:
  124.7 99.7 all-gather.6
  226.3 69.0 all-gather.8
  297.2 35.0 all-gather.12
  334.6 93.6 all-gather.10

commit v2 on v0

--- a/solution.py
+++ b/solution.py
@@ -38,7 +38,9 @@
     mean = lax.psum(jnp.sum(values, axis=1), "col")[:, None] / D
     spread = lax.psum(jnp.sum((values - mean) ** 2, axis=1), "col")
     payload = normalize(values, mean, spread[:, None] / D, gain_part, bias_part)
-    gathered = lax.all_gather(payload, "col", axis=1, tiled=True)
+    gathered = jnp.concatenate(
+        lax.all_to_all(jnp.stack([payload] * lax.axis_size("col")), "col", 0, 0), axis=1
+    )
     left = gathered
     qkv = jnp.dot(
         left, lax.all_gather(w_qkv, "row", axis=0, tiled=True), preferred_element_type=jnp.float32

time: 466 us -> 403 us (0.86)
  waiting for transfers between devices: 290 us -> 196 us
  starting transfers between devices: 0.12 us -> 23.4 us
    all_gather x1 -> x0, waiting for transfers between devices: 98.9 us -> none  [on_device(): gathered = lax.all_gather(payload, 'col', axis=1, tiled=True)]
    all_to_all x0 -> x1, waiting for transfers between devices: none -> 98 us  [on_device(): lax.all_to_all(jnp.stack([payload] * lax.axis_size('col')), 'col', 0, 0)]
    all_gather x1, waiting for transfers between devices: 70.9 us -> 0.01 us  [on_device(): lax.all_gather(w_qkv, 'row', axis=0, tiled=True)]
    all_to_all x0 -> x1, starting transfers between devices: none -> 23.3 us  [on_device(): lax.all_to_all(jnp.stack([payload] * lax.axis_size('col')), 'col', 0, 0)]
    all_gather x1, waiting for transfers between devices: 22.6 us -> 0.02 us  [on_device(): lax.all_gather(w_out, 'row', axis=0, tiled=True)]
  transfers between devices with their start and end apart: 4 -> 4, of which waited for: 4 -> 2; matrix products, arithmetic and copies ran while one was open for 3% -> 6% of each run, Pallas kernels for 0% -> 0%
where the time goes in v2:
time: 403 us
  waiting for transfers between devices  196 us (49%)
  blocking collectives  140 us (35%)
  starting transfers between devices  23.4 us (6%)
  matrix products  18.8 us (5%)
  between operations  13.2 us (3%)
  local copies, waits for them, and re-layouts  7.84 us (2%)
    all_to_all x1, waiting for transfers between devices, on_device(): lax.all_to_all(jnp.stack([payload] * lax.axis_size('col')), 'col', 0, 0)  98 us
    all_gather x1, waiting for transfers between devices, on_device(): full_context = lax.all_gather(context, 'col', axis=1, tiled=True)  96.9 us
    psum x1, blocking collectives, on_device(): spread = lax.psum(jnp.sum((values - mean) ** 2, axis=1), 'col')  73.2 us
    psum x1, blocking collectives, on_device(): mean = lax.psum(jnp.sum(values, axis=1), 'col')[:, None] / D  66.9 us
    all_to_all x1, starting transfers between devices, on_device(): lax.all_to_all(jnp.stack([payload] * lax.axis_size('col')), 'col', 0, 0)  23.3 us
    dot_general x1, matrix products, on_device(): jnp.dot(left, lax.all_gather(w_qkv, 'row', axis=0, tiled=True), preferred...  11.5 us
  transfers between devices with their start and end apart: 4, of which 2 were waited for; matrix products, arithmetic and copies ran while one was open for 6% of the time, Pallas kernels for 0%

profile of v2, /device:TPU:36, one launch (start us, length us, event | category | flops | bytes accessed | tf_op | source)
XLA Modules:
  0.0 403.1 jit_solution(5428748751274947983)
XLA Ops:
  6.5 0.7 all-gather.4.cloned.1.call-update
  7.3 0.8 dynamic_slice.6
  8.0 0.8 dynamic_slice.7
  8.8 1.1 convert_reduce_fusion
  9.9 66.9 %psum.14 = f32[384]{0:T(512)S(1)} all-reduce(f32[384]{0:T(512)S(1)} %convert_reduce_fusion), channel_id=1, replica_groups=mesh['row'=8,'col'=32] {'col'}, use_global_device_ids=true, to_apply=%region_1.0 | all-reduce | flops 384 | bytes 3072 | tf_op jit(solution)/shard_map/psum | solution.py:38
  76.8 1.2 fusion.7
  77.9 73.2 %psum.15 = f32[384]{0:T(512)S(1)} all-reduce(f32[384]{0:T(512)S(1)} %fusion.7), channel_id=1, replica_groups=mesh['row'=8,'col'=32] {'col'}, use_global_device_ids=true, to_apply=%region_3.0 | all-reduce | flops 384 | bytes 3072 | tf_op jit(solution)/shard_map/psum | solution.py:39
  151.1 1.1 fusion.10
  152.3 0.2 copy.11
  152.4 3.5 stack.2
  156.0 23.3 %all-to-all-start = ((bf16[32,384,256]{1,2,0:T(8,128)(2,1)}), bf16[32,384,256]{1,2,0:T(8,128)(2,1)}, u32[]{:S(2)}, u32[]{:S(2)}) async-start(bf16[32,384,256]{1,2,0:T(8,128)(2,1)} %stack.2), calls=%async_computation | async-start | bytes 12582912 | tf_op jit(solution)/shard_map/all_to_all | solution.py:42
  179.3 0.7 all-gather.8.cloned.1.call-update
  180.1 98.0 %all-to-all-done = bf16[32,384,256]{1,2,0:T(8,128)(2,1)} async-done(((bf16[32,384,256]{1,2,0:T(8,128)(2,1)}), bf16[32,384,256]{1,2,0:T(8,128)(2,1)}, u32[]{:S(2)}, u32[]{:S(2)}) %all-to-all-start) | async-done | bytes 6291488 | tf_op jit(solution)/shard_map/all_to_all | solution.py:42
  278.1 11.5 %convolution_convert_fusion = bf16[384,768]{1,0:T(8,128)(2,1)S(1)} fusion(bf16[384,8192]{0,1:T(8,128)(2,1)} %bitcast.1, bf16[8192,768]{1,0:T(8,128)(2,1)} %all-gather.4.cloned.1.call-done), kind=kOutput, calls=%fused_computation.1 | convolution fusion | flops 4832133120 | bytes 19464192 | tf_op jit(solution)/shard_map/dot_general | solution.py:45
  289.6 0.3 reshape.27
  289.9 0.9 fusion.15
  290.7 0.6 copy.18
  291.3 0.3 fusion.16
  291.7 0.3 convolution_multiply_fusion
  291.9 0.3 fusion.4
  292.2 0.2 copy.16
  292.4 0.7 copy.35
  293.1 96.9 %all-gather.6.cloned.1.call-done = bf16[384,8192]{1,0:T(8,128)(2,1)} async-done(((bf16[384,256]{1,0:T(8,128)(2,1)}), bf16[384,8192]{1,0:T(8,128)(2,1)}) %all-gather.6.cloned.1.call-update) | async-done | bytes 6291472 | tf_op jit(solution)/shard_map/all_gather | solution.py:49
  390.1 6.5 %fusion.3 = bf16[384,256]{1,0:T(8,128)(2,1)} fusion(bf16[384,8192]{1,0:T(8,128)(2,1)} %all-gather.6.cloned.1.call-done, bf16[8192,256]{1,0:T(8,128)(2,1)} %all-gather.8.cloned.1.call-done, f32[256]{0:T(256)S(1)} %copy-done), kind=kOutput, calls=%fused_computation.6 | convolution fusion | flops 1610809344 | bytes 10683392 | tf_op jit(solution)/shard_map/dot_general | solution.py:51
  (10 shorter events, 0.1 us)
Async XLA Ops:
  6.5 271.6 %all-gather.4.cloned.1.call-start = ((), (), s32[]{:S(2)}) async-start(), calls=%async_computation.1 | async-start | bytes 14155776 | tf_op jit(solution)/shard_map/all_gather | solution.py:46
  156.0 122.1 %all-to-all-start = ((bf16[32,384,256]{1,2,0:T(8,128)(2,1)}), bf16[32,384,256]{1,2,0:T(8,128)(2,1)}, u32[]{:S(2)}, u32[]{:S(2)}) async-start(bf16[32,384,256]{1,2,0:T(8,128)(2,1)} %stack.2), calls=%async_computation | async-start | bytes 12582912 | tf_op jit(solution)/shard_map/all_to_all | solution.py:42
  179.3 113.8 %all-gather.8.cloned.1.call-start = ((), (), s32[]{:S(2)}) async-start(), calls=%async_computation.3 | async-start | bytes 4718592 | tf_op jit(solution)/shard_map/all_gather | solution.py:52
  180.1 210.0 %all-gather.6.cloned.1.call-start = ((), (), s32[]{:S(2)}) async-start(), calls=%async_computation.2 | async-start | bytes 6488064 | tf_op jit(solution)/shard_map/all_gather | solution.py:49
  289.6 100.5 %copy-start = (f32[256]{0:T(256)S(1)}, f32[256]{0:T(256)}, u32[]{:S(2)}) copy-start(f32[256]{0:T(256)} %param.11) | copy-start | bytes 3076
Sparse Core Ops, SparseCore 0:
  9.2 72.3 all-gather.3
  182.0 35.8 all-gather.7
  293.2 96.7 all-gather.5
